TPU v7x, 256 devices: a whole 4x4x8 slice. The times are simulated.
256 devices in a mesh: ctx: 32 (over z_hi, y, x), ch: 8 (over z_lo, core).
Axes of the slice: x: 4, y: 4, z: 8 (z_hi: 2, z_lo: 4; z = z_hi * 4 + z_lo), core: 2. Of those that a mesh axis runs over, the one named last changes fastest.
Arguments:
- grad_out: bfloat16 [24576, 4096], P('ctx', 'ch'), may hold values from -6 to 6
- block_input: bfloat16 [24576, 4096], P('ctx', 'ch'), may hold values from -40 to 40
- norm_gain: bfloat16 [4096], P('ch'), may hold values from 0.5 to 1.5
- queries: bfloat16 [24576, 4096], P('ctx', 'ch'), may hold values from -6 to 6
- keys: bfloat16 [24576, 4096], P('ctx', 'ch'), may hold values from -6 to 6
- values: bfloat16 [24576, 4096], P('ctx', 'ch'), may hold values from -6 to 6
- filters: bfloat16 [256, 128], P('ch'), may hold values from -0.5 to 0.5
- doc_starts: int32 [32, 4], P('ctx'), may hold values from 0 to 767, as said below
- in_weight: bfloat16 [4096, 3, 4096], P('ctx', None, 'ch'), may hold values from -0.09375 to 0.09375
- out_weight: bfloat16 [4096, 4096], P('ch', 'ctx'), may hold values from -0.09375 to 0.09375
Outputs:
- grad_input: bfloat16 [24576, 4096], P('ctx', 'ch')
Inputs may be any that keep to these rules, and one draw needn't show every extreme that they name: `doc_starts`: each row holds 4 distinct document starts of one slab as offsets within the slab, in ascending order; the first slab's first start is 0.
All inputs are finite; a program needn't handle non-finite values.
Results may differ from a plain program's by a relative error of at most 0.013.
Values may be sent and summed in bfloat16 or wider, within the bound.
A program may use at most 128 MiB of HBM per device.

v0:
```python
import jax
import jax.numpy as jnp
from jax import lax
from jax.sharding import PartitionSpec as P

D = 4096
FILTER_LEN = 128
GROUP_WIDTH = 16
DOCS = 4
epsilon = 1e-05


def shifted(block, axis, distance):
    devices = range(lax.axis_size(axis))
    route = [(i - distance, i) for i in devices if i - distance in devices]
    return lax.ppermute(block, axis, route)


def on_device(
    grad_out,
    block_input,
    norm_gain,
    queries,
    keys,
    values,
    filters,
    doc_starts,
    in_weight,
    out_weight,
):
    tok_rows = grad_out.shape[0]
    chan_width = grad_out.shape[1]
    group_count = filters.shape[0]
    tile_count = tok_rows // FILTER_LEN
    source_in = block_input.astype(jnp.float32)
    square_sum = lax.psum(jnp.sum(source_in * source_in, axis=1), "ch")
    starts = doc_starts[0]
    positions = jnp.arange(tok_rows, dtype=jnp.int32)
    own_last = jnp.max(
        jnp.where(starts[None, :] <= positions[:, None], starts[None, :], -tok_rows), axis=1
    )
    products = (keys.astype(jnp.float32) * values.astype(jnp.float32)).astype(jnp.bfloat16)
    tail_rows, prior_start = shifted(
        (products[tok_rows - FILTER_LEN :], starts[DOCS - 1 :]), "ctx", 1
    )
    last_start = jnp.maximum(own_last, prior_start[0] - tok_rows)
    tap_index = (
        jnp.arange(FILTER_LEN, dtype=jnp.int32)[:, None]
        + FILTER_LEN
        - jnp.arange(2 * FILTER_LEN, dtype=jnp.int32)[None, :]
    )
    selector = (jnp.arange(FILTER_LEN, dtype=jnp.int32)[:, None, None] == tap_index[None]).astype(
        jnp.bfloat16
    )
    selector = selector.reshape(FILTER_LEN, 2 * FILTER_LEN * FILTER_LEN)
    table = jnp.dot(filters, selector, preferred_element_type=jnp.float32).astype(jnp.bfloat16)
    table = table.reshape(group_count, FILTER_LEN, 2 * FILTER_LEN)
    flipped = table[:, ::-1, ::-1]
    padded_prod = jnp.concatenate([tail_rows, products], axis=0)

    def forward_tile(tile_idx):
        source = lax.dynamic_slice_in_dim(padded_prod, tile_idx * FILTER_LEN, 2 * FILTER_LEN, 0)
        source = source.reshape(2 * FILTER_LEN, group_count, GROUP_WIDTH)
        row_last = lax.dynamic_slice_in_dim(last_start, tile_idx * FILTER_LEN, FILTER_LEN, 0)
        col_pos = (tile_idx - 1) * FILTER_LEN + jnp.arange(2 * FILTER_LEN, dtype=jnp.int32)
        allowed = col_pos[None, :] >= row_last[:, None]
        masked = jnp.where(allowed[None], table, jnp.zeros_like(table))
        return jnp.einsum(
            "gtp,pgc->tgc", masked, source, preferred_element_type=jnp.float32
        ).reshape(FILTER_LEN, chan_width)

    mixed = lax.map(forward_tile, jnp.arange(tile_count, dtype=jnp.int32)).reshape(
        tok_rows, chan_width
    )
    gathered = lax.all_gather(grad_out, "ch", axis=1, tiled=True)
    mix_grad = lax.dot_general(
        gathered,
        lax.all_gather(out_weight, "ctx", axis=1, tiled=True),
        (((1,), (1,)), ((), ())),
        preferred_element_type=jnp.float32,
    )
    q_grad = (mix_grad * mixed).astype(jnp.bfloat16)
    w_grad = (mix_grad * queries.astype(jnp.float32)).astype(jnp.bfloat16)
    head_rows, head_last = shifted((w_grad[:FILTER_LEN], last_start[:FILTER_LEN]), "ctx", -1)
    padded_grad = jnp.concatenate([w_grad, head_rows], axis=0)
    padded_last = jnp.concatenate([last_start, head_last + tok_rows], axis=0)

    def backward_tile(tile_idx):
        source = lax.dynamic_slice_in_dim(padded_grad, tile_idx * FILTER_LEN, 2 * FILTER_LEN, 0)
        source = source.reshape(2 * FILTER_LEN, group_count, GROUP_WIDTH)
        col_last = lax.dynamic_slice_in_dim(padded_last, tile_idx * FILTER_LEN, 2 * FILTER_LEN, 0)
        row_pos = tile_idx * FILTER_LEN + jnp.arange(FILTER_LEN, dtype=jnp.int32)
        allowed = row_pos[:, None] >= col_last[None, :]
        masked = jnp.where(allowed[None], flipped, jnp.zeros_like(flipped))
        return jnp.einsum(
            "gst,tgc->sgc", masked, source, preferred_element_type=jnp.float32
        ).reshape(FILTER_LEN, chan_width)

    conv_grad = lax.map(backward_tile, jnp.arange(tile_count, dtype=jnp.int32)).reshape(
        tok_rows, chan_width
    )
    k_grad = (conv_grad * values.astype(jnp.float32)).astype(jnp.bfloat16)
    v_grad = (conv_grad * keys.astype(jnp.float32)).astype(jnp.bfloat16)
    stacked = jnp.stack([q_grad, k_grad, v_grad], axis=1).reshape(tok_rows, 3 * chan_width)
    weight_rows = lax.all_gather(in_weight, "ctx", axis=0, tiled=True)
    flat_rows = weight_rows.reshape(weight_rows.shape[0], 3 * chan_width)
    hidden_terms = lax.dot_general(
        stacked, flat_rows, (((1,), (1,)), ((), ())), preferred_element_type=jnp.float32
    )
    norm_grad = lax.psum_scatter(
        hidden_terms.astype(jnp.bfloat16), "ch", scatter_dimension=1, tiled=True
    ).astype(jnp.float32)
    scaled = norm_gain.astype(jnp.float32)[None, :] * norm_grad
    cross_sum = lax.psum(jnp.sum(scaled * source_in, axis=1), "ch")
    inverse = lax.rsqrt(square_sum / D + epsilon)[:, None]
    result = (
        grad_out.astype(jnp.float32)
        + inverse * scaled
        - source_in * (inverse * inverse * inverse) * cross_sum[:, None] / D
    )
    return result.astype(jnp.bfloat16)


def solution(mesh):
    placed = (
        P("ctx", "ch"),
        P("ctx", "ch"),
        P("ch"),
        P("ctx", "ch"),
        P("ctx", "ch"),
        P("ctx", "ch"),
        P("ch", None),
        P("ctx", None),
        P("ctx", None, "ch"),
        P("ch", "ctx"),
    )
    return jax.shard_map(
        on_device, mesh=mesh, in_specs=placed, out_specs=P("ctx", "ch"), check_vma=False
    )
```

profile of v0, /device:TPU:1, one launch (start us, length us, event | category | flops | bytes accessed | tf_op | source)
XLA Modules:
  0.0 529.9 jit_solution(16419598484490058867)
XLA Ops:
  6.5 0.7 all-gather.6.cloned.1.call-update
  7.3 0.7 all-gather.4.cloned.1.call-update
  8.1 0.7 all-gather.8.cloned.1.call-update
  8.8 1.3 fusion.17
  10.2 3.9 collective-permute-start
  14.1 0.6 slice.16
  14.7 3.6 collective-permute-start.1
  18.7 3.5 convolution_convert_fusion
  22.2 0.5 copy.28
  22.7 22.6 %rev.3 = bf16[32,128,256]{2,1,0:T(8,128)(2,1)} reverse(bf16[32,128,256]{2,1,0:T(8,128)(2,1)S(1)} %bitcast.57), dimensions={1,2} | reverse | bytes 4194304 | tf_op jit(solution)/shard_map/rev | solution.py:58
  46.0 1.3 collective-permute-start.3
  47.3 1.0 pad_maximum_fusion
  48.3 1.4 broadcast.91.clone2
  49.7 28.5 %while.22 = (s32[]{:T(128)}, f32[6,128,512]{2,1,0:T(8,128)}, s32[6]{0:T(128)S(1)}, bf16[896,512]{1,0:T(8,128)(2,1)}, s32[768]{0:T(1024)S(1)}, /*index=5*/bf16[32...) while((s32[]{:T(128)}, f32[6,128,512]{2,1,0:T(8,128)}, ...), condition=%wide.region_4.5_spmd, body=%wide.region_3.4_spmd.sunk | while | flops 34636040 | bytes 4788460 | solution.py:72
  49.7 0.6 dynamic_slice.37
  51.8 1.0 constant_dynamic-slice_fusion.4
  52.9 0.6 fusion.41
  53.7 0.7 constant_dynamic-update-slice_fusion.4
  54.4 0.6 dynamic_slice.37
  56.5 1.0 constant_dynamic-slice_fusion.4
  57.7 0.6 fusion.41
  58.5 0.7 constant_dynamic-update-slice_fusion.4
  59.2 0.6 dynamic_slice.37
  61.3 1.0 constant_dynamic-slice_fusion.4
  62.4 0.6 fusion.41
  63.2 0.7 constant_dynamic-update-slice_fusion.4
  63.9 0.6 dynamic_slice.37
  66.0 1.0 constant_dynamic-slice_fusion.4
  67.2 0.7 fusion.41
  68.0 0.7 constant_dynamic-update-slice_fusion.4
  68.7 0.6 dynamic_slice.37
  70.8 1.0 constant_dynamic-slice_fusion.4
  71.9 0.6 fusion.41
  72.7 0.7 constant_dynamic-update-slice_fusion.4
  73.4 0.6 dynamic_slice.37
  75.5 1.0 constant_dynamic-slice_fusion.4
  76.6 0.6 fusion.41
  77.4 0.7 constant_dynamic-update-slice_fusion.4
  78.2 68.1 %all-gather.6.cloned.1.call-done = bf16[512,4096]{1,0:T(8,128)(2,1)} async-done(((bf16[512,128]{1,0:T(8,128)(2,1)}), bf16[512,4096]{1,0:T(8,128)(2,1)}) %all-gather.6.cloned.1.call-update) | async-done | bytes 4194320 | tf_op jit(solution)/shard_map/all_gather | solution.py:78
  146.2 71.0 %all-gather.4.cloned.1.call-done = bf16[768,4096]{1,0:T(8,128)(2,1)} async-done(((bf16[768,512]{1,0:T(8,128)(2,1)}), bf16[768,4096]{1,0:T(8,128)(2,1)}) %all-gather.4.cloned.1.call-update) | async-done | bytes 6291472 | tf_op jit(solution)/shard_map/all_gather | solution.py:75
  217.3 9.0 %fusion.25 = (bf16[768,512]{1,0:T(8,128)(2,1)}, bf16[768,512]{1,0:T(8,128)(2,1)S(1)}) fusion(f32[6,128,512]{2,1,0:T(8,128)} %get-tuple-element.114, bf16[768,512]{1,0:T(8,128)(2,1)} %param.17, bf16[768,4096]{1,0:T(8,128)(2,1)} %all-gather.4.cloned.1.call-done, bf16[512,4096]{1,0:T(8,128)(2,1)} %all-gather.6.cloned.1.call-done), kind=kOutput, calls=%fused_computation.43 | convolution fusion | flops 3223191552 | bytes 14417920 | tf_op jit(solution)/shard_map/dot_general | solution.py:76
  226.3 1.5 collective-permute-start.2
  227.8 4.2 collective-permute-done.2
  232.2 23.9 %while.23 = (s32[]{:T(128)}, f32[6,128,512]{2,1,0:T(8,128)S(1)}, s32[6]{0:T(128)S(1)}, bf16[896,512]{1,0:T(8,128)(2,1)S(1)}, s32[896]{0:T(1024)S(1)}, /*index=5*...) while((s32[]{:T(128)}, f32[6,128,512]{2,1,0:T(8,128)S(1)}, s32[6]{0:T(128)S(1)}, ...), condition=%wide.region_6.7_spmd, body=%wide.region_5.6_spmd.sunk | while | flops 34635908 | bytes 4788399 | solution.py:99
  232.2 0.6 dynamic_slice.40
  233.8 2.4 fusion.44
  236.3 0.6 dynamic_slice.40
  237.8 2.2 fusion.44
  240.3 0.6 dynamic_slice.40
  241.8 2.2 fusion.44
  244.2 0.6 dynamic_slice.40
  245.7 2.2 fusion.44
  248.2 0.6 dynamic_slice.40
  249.7 2.2 fusion.44
  252.2 0.6 dynamic_slice.40
  253.7 2.2 fusion.44
  256.1 1.8 fusion.18
  257.9 163.2 %all-gather.8.cloned.1.call-done = bf16[4096,3,512]{2,0,1:T(8,128)(2,1)} async-done(((bf16[128,3,512]{2,0,1:T(8,128)(2,1)}), bf16[4096,3,512]{2,0,1:T(8,128)(2,1)}) %all-gather.8.cloned.1.call-update) | async-done | bytes 12582928 | tf_op jit(solution)/shard_map/all_gather | solution.py:105
  421.1 14.8 %bitcast_convert_fusion = bf16[768,4096]{1,0:T(8,128)(2,1)} fusion(bf16[4096,3,512]{2,0,1:T(8,128)(2,1)} %all-gather.8.cloned.1.call-done, bf16[768,1,512]{2,0,1:T(8,128)(2,1)S(1)} %bitcast.65, bf16[768,1,512]{2,0,1:T(8,128)(2,1)S(1)} %bitcast.64, bf16[768,1,512]{2,0,1:T(8,128)(2,1)} %bitcast.69), kind=kOutput, calls=%fused_computation.20 | convolution fusion | flops 9669181440 | bytes 21233664 | tf_op jit(solution)/shard_map/dot_general | solution.py:107
  435.9 0.7 copy-done.5
  436.5 67.7 %reduce-scatter.2.cloned.1.call-done = bf16[768,512]{1,0:T(8,128)(2,1)} async-done(((bf16[768,4096]{1,0:T(8,128)(2,1)}), bf16[768,512]{1,0:T(8,128)(2,1)}) %reduce-scatter.2.cloned.1.call-update) | async-done | bytes 786448 | tf_op jit(solution)/shard_map/reduce_scatter | solution.py:110
  504.3 1.6 fusion.19
  505.9 16.0 %all-reduce = (f32[768]{0:T(1024)S(1)}, f32[768]{0:T(1024)S(1)}) all-reduce(f32[768]{0:T(1024)S(1)} %get-tuple-element.141, f32[768]{0:T(1024)S(1)} %get-tuple-element.140), channel_id=1, replica_groups=mesh['ctx'=32,'ch'=8] {'ch'}, use_global_device_ids=true, to_apply=%region_9.10 | all-reduce | flops 1536 | bytes 12288 | tf_op jit(solution)/shard_map/psum | solution.py:114
  521.9 1.5 fusion.23
  (111 shorter events, 6.6 us)
Async XLA Ops:
  6.5 12.1 %copy-start = (bf16[32,128]{1,0:T(8,128)(2,1)S(1)}, bf16[32,128]{1,0:T(8,128)(2,1)}, u32[]{:S(2)}) copy-start(bf16[32,128]{1,0:T(8,128)(2,1)} %param.20) | copy-start | bytes 24580
  6.5 2.3 copy-start.1
  6.5 139.7 %all-gather.6.cloned.1.call-start = ((), (), s32[]{:S(2)}) async-start(), calls=%async_computation.2 | async-start | bytes 4325376 | tf_op jit(solution)/shard_map/all_gather | solution.py:78
  7.3 210.0 %all-gather.4.cloned.1.call-start = ((), (), s32[]{:S(2)}) async-start(), calls=%async_computation.1 | async-start | bytes 7077888 | tf_op jit(solution)/shard_map/all_gather | solution.py:75
  8.0 6.1 %copy-start.6 = (s32[1,4]{1,0:T(1,128)S(1)}, s32[1,4]{1,0:T(1,128)}, u32[]{:S(2)}) copy-start(s32[1,4]{1,0:T(1,128)} %param.21) | copy-start | bytes 52
  8.0 413.0 %all-gather.8.cloned.1.call-start = ((), (), s32[]{:S(2)}) async-start(), calls=%async_computation.3 | async-start | bytes 12976128 | tf_op jit(solution)/shard_map/all_gather | solution.py:105
  8.8 495.5 %reduce-scatter.2.cloned.1.call-start = ((), (), s32[]{:S(2)}) async-start(), calls=%async_computation.4 | async-start | bytes 7077888 | tf_op jit(solution)/shard_map/reduce_scatter | solution.py:110
  10.2 37.1 %collective-permute-start = (bf16[128,512]{1,0:T(8,128)(2,1)S(1)}, bf16[128,512]{1,0:T(8,128)(2,1)S(1)}, u32[]{:S(2)}, u32[]{:S(2)}) collective-permute-start(bf16[128,512]{1,0:T(8,128)(2,1)S(1)} %slice.20), channel_id=1, source_target_pairs={{0,8},{8,16},{16,24},{24,32},{32,40},{40,48},{48,56},{56,64},{64,7... | collective-permute-start | bytes 393224 | tf_op jit(solution)/shard_map/ppermute | solution.py:16
  14.7 30.6 %collective-permute-start.1 = (s32[1]{0:T(128)}, s32[1]{0:T(128)}, u32[]{:S(2)}, u32[]{:S(2)}) collective-permute-start(s32[1]{0:T(128)} %bitcast.10), channel_id=1, source_target_pairs={{0,8},{8,16},{16,24},{24,32},{32,40},{40,48},{48,56},{56,64},{64,7... | collective-permute-start | bytes 20 | tf_op jit(solution)/shard_map/ppermute | solution.py:16
  46.0 181.8 %collective-permute-start.3 = (s32[128]{0:T(128)S(1)}, s32[128]{0:T(128)S(1)}, u32[]{:S(2)}, u32[]{:S(2)}) collective-permute-start(s32[128]{0:T(128)S(1)} %slice.19), channel_id=1, source_target_pairs={{8,0},{16,8},{24,16},{32,24},{40,32},{48,40},{56,48},{64,56},{72,6... | collective-permute-start | bytes 1544 | tf_op jit(solution)/shard_map/ppermute | solution.py:16
  226.3 5.7 %collective-permute-start.2 = (bf16[128,512]{1,0:T(8,128)(2,1)S(1)}, bf16[128,512]{1,0:T(8,128)(2,1)S(1)}, u32[]{:S(2)}, u32[]{:S(2)}) collective-permute-start(bf16[128,512]{1,0:T(8,128)(2,1)S(1)} %slice.21), channel_id=1, source_target_pairs={{8,0},{16,8},{24,16},{32,24},{40,32},{48,40},{56,48},{64,56},{72,6... | collective-permute-start | bytes 393224 | tf_op jit(solution)/shard_map/ppermute | solution.py:16
  435.8 0.7 copy-start.5
  435.8 68.4 %copy-start.2 = (bf16[768,512]{1,0:T(8,128)(2,1)S(1)}, bf16[768,512]{1,0:T(8,128)(2,1)}, u32[]{:S(2)}) copy-start(bf16[768,512]{1,0:T(8,128)(2,1)} %param.15) | copy-start | bytes 2359300
  436.5 85.4 %copy-start.3 = (bf16[768,512]{1,0:T(8,128)(2,1)S(1)}, bf16[768,512]{1,0:T(8,128)(2,1)}, u32[]{:S(2)}) copy-start(bf16[768,512]{1,0:T(8,128)(2,1)} %param.14) | copy-start | bytes 2359300
  504.3 17.7 %copy-start.4 = (bf16[768,512]{1,0:T(8,128)(2,1)S(1)}, bf16[768,512]{1,0:T(8,128)(2,1)}, u32[]{:S(2)}) copy-start(bf16[768,512]{1,0:T(8,128)(2,1)} %reduce-scatter.2.cloned.1.call-done) | copy-start | bytes 2359300
Sparse Core Ops, SparseCore 0:
  10.5 135.6 all-gather.5
  148.0 69.2 all-gather.3
  220.8 200.1 all-gather.7
  436.0 68.2 reduce-scatter.1
where the time goes:
time: 531 us; the launch traced here: 530 us
  waiting for transfers between devices  376 us (71%)
  local copies, waits for them, and re-layouts  48.3 us (9%)
  matrix products  44.6 us (8%)
  blocking collectives  16 us (3%)
  between operations  13.9 us (3%)
  loops' own time  11.8 us (2%)
  starting transfers between devices  10.4 us (2%)
  other arithmetic  8.54 us (2%)
    all_gather x1, waiting for transfers between devices, on_device(): weight_rows = lax.all_gather(in_weight, 'ctx', axis=0, tiled=True)  163 us
    all_gather x1, waiting for transfers between devices, on_device(): gathered = lax.all_gather(grad_out, 'ch', axis=1, tiled=True)  71 us
    all_gather x1, waiting for transfers between devices, on_device(): lax.all_gather(out_weight, 'ctx', axis=1, tiled=True)  68.1 us
    reduce_scatter x1, waiting for transfers between devices, on_device(): lax.psum_scatter(hidden_terms.astype(jnp.bfloat16), 'ch', scatter_dimensi...  67.7 us
    rev x1, local copies, waits for them, and re-layouts, on_device(): flipped = table[:, ::-1, ::-1]  22.6 us
    psum x1, blocking collectives, on_device(): cross_sum = lax.psum(jnp.sum(scaled * source_in, axis=1), 'ch')  16 us
    dot_general x1, matrix products, on_device(): lax.dot_general(stacked, flat_rows, (((1,), (1,)), ((), ())), preferred_e...  14.8 us
    dot_general x6, matrix products, backward_tile(): jnp.einsum('gst,tgc->sgc', masked, source, preferred_element_type=jnp.flo...  13.6 us
  transfers between devices with their start and end apart: 8, of which 5 were waited for; matrix products, arithmetic and copies ran while one was open for 16% of the time, Pallas kernels for 0%

commit v1 on v0

--- a/solution.py
+++ b/solution.py
@@ -73,9 +73,17 @@
         tok_rows, chan_width
     )
     gathered = lax.all_gather(grad_out, "ch", axis=1, tiled=True)
+
+    def _carry_series(patch, chip_axis):
+        v1 = jnp.concatenate(
+            lax.all_to_all(jnp.stack(lax.axis_size(chip_axis) * [patch], axis=0), chip_axis, 0, 0),
+            axis=1,
+        )
+        return v1
+
     mix_grad = lax.dot_general(
         gathered,
-        lax.all_gather(out_weight, "ctx", axis=1, tiled=True),
+        _carry_series(out_weight, "ctx"),
         (((1,), (1,)), ((), ())),
         preferred_element_type=jnp.float32,
     )

time: 531 us -> 491 us (0.925)
  waiting for transfers between devices: 376 us -> 318 us
  starting transfers between devices: 10.4 us -> 24.3 us
    all_to_all x0 -> x1, waiting for transfers between devices: none -> 71.6 us  [_carry_series(): lax.all_to_all(jnp.stack(lax.axis_size(chip_axis) * [patch], axis=0), chi...]
    all_gather x1 -> x0, waiting for transfers between devices: 68.1 us -> none  [on_device(): lax.all_gather(out_weight, 'ctx', axis=1, tiled=True)]
    all_gather x1, waiting for transfers between devices: 71 us -> 8.81 us  [on_device(): gathered = lax.all_gather(grad_out, 'ch', axis=1, tiled=True)]
    all_to_all x0 -> x1, starting transfers between devices: none -> 14.7 us  [_carry_series(): lax.all_to_all(jnp.stack(lax.axis_size(chip_axis) * [patch], axis=0), chi...]
  transfers between devices with their start and end apart: 8 -> 8, of which waited for: 5 -> 5; matrix products, arithmetic and copies ran while one was open for 16% -> 18% of each run, Pallas kernels for 0% -> 0%
where the time goes in v1:
time: 491 us; the launch traced here: 490 us
  waiting for transfers between devices  318 us (65%)
  local copies, waits for them, and re-layouts  52.5 us (11%)
  matrix products  44.6 us (9%)
  starting transfers between devices  24.3 us (5%)
  blocking collectives  16 us (3%)
  between operations  14 us (3%)
  loops' own time  12.7 us (3%)
  other arithmetic  7.38 us (2%)
    all_gather x1, waiting for transfers between devices, on_device(): weight_rows = lax.all_gather(in_weight, 'ctx', axis=0, tiled=True)  164 us
    all_to_all x1, waiting for transfers between devices, _carry_series(): lax.all_to_all(jnp.stack(lax.axis_size(chip_axis) * [patch], axis=0), chi...  71.6 us
    reduce_scatter x1, waiting for transfers between devices, on_device(): lax.psum_scatter(hidden_terms.astype(jnp.bfloat16), 'ch', scatter_dimensi...  67.7 us
    rev x1, local copies, waits for them, and re-layouts, on_device(): flipped = table[:, ::-1, ::-1]  22.6 us
    psum x1, blocking collectives, on_device(): cross_sum = lax.psum(jnp.sum(scaled * source_in, axis=1), 'ch')  16 us
    dot_general x1, matrix products, on_device(): lax.dot_general(stacked, flat_rows, (((1,), (1,)), ((), ())), preferred_e...  14.8 us
    all_to_all x1, starting transfers between devices, _carry_series(): lax.all_to_all(jnp.stack(lax.axis_size(chip_axis) * [patch], axis=0), chi...  14.7 us
    dot_general x6, matrix products, backward_tile(): jnp.einsum('gst,tgc->sgc', masked, source, preferred_element_type=jnp.flo...  13.6 us
  transfers between devices with their start and end apart: 8, of which 5 were waited for; matrix products, arithmetic and copies ran while one was open for 18% of the time, Pallas kernels for 0%

profile of v1, /device:TPU:1, one launch (start us, length us, event | category | flops | bytes accessed | tf_op | source)
XLA Modules:
  0.0 489.7 jit_solution(8426792551903206693)
XLA Ops:
  6.5 0.7 all-gather.3.cloned.1.call-update
  7.3 0.7 all-gather.5.cloned.1.call-update
  8.0 1.0 copy.20
  9.0 2.5 stack.10
  11.5 14.7 %all-to-all-start = ((bf16[32,512,128]{1,2,0:T(8,128)(2,1)}), bf16[32,512,128]{1,2,0:T(8,128)(2,1)}, u32[]{:S(2)}, u32[]{:S(2)}) async-start(bf16[32,512,128]{1,2,0:T(8,128)(2,1)} %stack.10), calls=%async_computation | async-start | bytes 8388608 | tf_op jit(solution)/shard_map/all_to_all | solution.py:79
  26.6 3.1 collective-permute-start
  29.7 0.7 slice.16
  30.3 3.6 collective-permute-start.1
  34.3 3.5 convolution_convert_fusion
  38.3 22.6 %rev.3 = bf16[32,128,256]{2,1,0:T(8,128)(2,1)} reverse(bf16[32,128,256]{2,1,0:T(8,128)(2,1)S(1)} %bitcast.60), dimensions={1,2} | reverse | bytes 4194304 | tf_op jit(solution)/shard_map/rev | solution.py:58
  61.7 1.3 collective-permute-start.3
  63.0 1.0 pad_maximum_fusion
  64.0 1.4 broadcast.93.clone2
  65.4 29.1 %while.22 = (s32[]{:T(128)}, f32[6,128,512]{2,1,0:T(8,128)}, s32[6]{0:T(128)S(1)}, bf16[896,512]{1,0:T(8,128)(2,1)}, s32[768]{0:T(1024)S(1)}, /*index=5*/bf16[32...) while((s32[]{:T(128)}, f32[6,128,512]{2,1,0:T(8,128)}, ...), condition=%wide.region_4.5_spmd, body=%wide.region_3.4_spmd.sunk | while | flops 34636040 | bytes 4788460 | solution.py:72
  65.4 0.7 dynamic_slice.37
  67.6 1.0 constant_dynamic-slice_fusion.4
  68.7 0.6 fusion.41
  69.5 0.7 constant_dynamic-update-slice_fusion.4
  70.3 0.7 dynamic_slice.37
  72.5 1.0 constant_dynamic-slice_fusion.4
  73.6 0.6 fusion.41
  74.4 0.7 constant_dynamic-update-slice_fusion.4
  75.1 0.7 dynamic_slice.37
  77.3 1.0 constant_dynamic-slice_fusion.4
  78.5 0.6 fusion.41
  79.3 0.7 constant_dynamic-update-slice_fusion.4
  80.0 0.7 dynamic_slice.37
  82.2 1.0 constant_dynamic-slice_fusion.4
  83.3 0.6 fusion.41
  84.1 0.7 constant_dynamic-update-slice_fusion.4
  84.8 0.7 dynamic_slice.37
  87.0 1.0 constant_dynamic-slice_fusion.4
  88.2 0.6 fusion.41
  89.0 0.7 constant_dynamic-update-slice_fusion.4
  89.7 0.7 dynamic_slice.37
  91.9 1.0 constant_dynamic-slice_fusion.4
  93.0 0.6 fusion.41
  93.8 0.7 constant_dynamic-update-slice_fusion.4
  94.5 71.6 %all-to-all-done = bf16[32,512,128]{1,2,0:T(8,128)(2,1)} async-done(((bf16[32,512,128]{1,2,0:T(8,128)(2,1)}), bf16[32,512,128]{1,2,0:T(8,128)(2,1)}, u32[]{:S(2)}, u32[]{:S(2)}) %all-to-all-start) | async-done | bytes 4194336 | tf_op jit(solution)/shard_map/all_to_all | solution.py:79
  166.1 8.8 %all-gather.3.cloned.1.call-done = bf16[768,4096]{1,0:T(8,128)(2,1)} async-done(((bf16[768,512]{1,0:T(8,128)(2,1)}), bf16[768,4096]{1,0:T(8,128)(2,1)}) %all-gather.3.cloned.1.call-update) | async-done | bytes 6291472 | tf_op jit(solution)/shard_map/all_gather | solution.py:75
  175.0 8.9 %fusion.25 = (bf16[768,512]{1,0:T(8,128)(2,1)}, bf16[768,512]{1,0:T(8,128)(2,1)S(1)}) fusion(f32[6,128,512]{2,1,0:T(8,128)} %get-tuple-element.114, bf16[768,512]{1,0:T(8,128)(2,1)} %param.17, bf16[768,4096]{1,0:T(8,128)(2,1)} %all-gather.3.cloned.1.call-done, bf16[512,4096]{0,1:T(8,128)(2,1)} %bitcast.10), kind=kOutput, calls=%fused_computation.43 | convolution fusion | flops 3223191552 | bytes 14417920 | tf_op jit(solution)/shard_map/dot_general | solution.py:84
  183.9 1.5 collective-permute-start.2
  185.4 4.2 collective-permute-done.2
  189.9 24.8 %while.23 = (s32[]{:T(128)}, f32[6,128,512]{2,1,0:T(8,128)S(1)}, s32[6]{0:T(128)S(1)}, bf16[896,512]{1,0:T(8,128)(2,1)S(1)}, s32[896]{0:T(1024)S(1)}, /*index=5*...) while((s32[]{:T(128)}, f32[6,128,512]{2,1,0:T(8,128)S(1)}, s32[6]{0:T(128)S(1)}, ...), condition=%wide.region_6.7_spmd, body=%wide.region_5.6_spmd.sunk | while | flops 34635908 | bytes 4788399 | solution.py:107
  189.9 0.7 dynamic_slice.40
  191.5 2.2 fusion.44
  194.0 0.7 dynamic_slice.40
  195.6 2.4 fusion.44
  198.2 0.7 dynamic_slice.40
  199.8 2.2 fusion.44
  202.3 0.7 dynamic_slice.40
  203.9 2.3 fusion.44
  206.4 0.7 dynamic_slice.40
  208.0 2.3 fusion.44
  210.6 0.7 dynamic_slice.40
  212.2 2.2 fusion.44
  214.6 1.8 fusion.18
  216.4 164.4 %all-gather.5.cloned.1.call-done = bf16[4096,3,512]{2,0,1:T(8,128)(2,1)} async-done(((bf16[128,3,512]{2,0,1:T(8,128)(2,1)}), bf16[4096,3,512]{2,0,1:T(8,128)(2,1)}) %all-gather.5.cloned.1.call-update) | async-done | bytes 12582928 | tf_op jit(solution)/shard_map/all_gather | solution.py:113
  380.8 14.8 %bitcast_convert_fusion = bf16[768,4096]{1,0:T(8,128)(2,1)} fusion(bf16[4096,3,512]{2,0,1:T(8,128)(2,1)} %all-gather.5.cloned.1.call-done, bf16[768,1,512]{2,0,1:T(8,128)(2,1)S(1)} %bitcast.68, bf16[768,1,512]{2,0,1:T(8,128)(2,1)S(1)} %bitcast.67, bf16[768,1,512]{2,0,1:T(8,128)(2,1)} %bitcast.72), kind=kOutput, calls=%fused_computation.20 | convolution fusion | flops 9669181440 | bytes 21233664 | tf_op jit(solution)/shard_map/dot_general | solution.py:115
  395.6 0.7 copy-done.6
  396.3 67.7 %reduce-scatter.2.cloned.1.call-done = bf16[768,512]{1,0:T(8,128)(2,1)} async-done(((bf16[768,4096]{1,0:T(8,128)(2,1)}), bf16[768,512]{1,0:T(8,128)(2,1)}) %reduce-scatter.2.cloned.1.call-update) | async-done | bytes 786448 | tf_op jit(solution)/shard_map/reduce_scatter | solution.py:118
  464.0 1.6 fusion.19
  465.6 16.0 %all-reduce = (f32[768]{0:T(1024)S(1)}, f32[768]{0:T(1024)S(1)}) all-reduce(f32[768]{0:T(1024)S(1)} %get-tuple-element.153, f32[768]{0:T(1024)S(1)} %get-tuple-element.152), channel_id=1, replica_groups=mesh['ctx'=32,'ch'=8] {'ch'}, use_global_device_ids=true, to_apply=%region_9.10 | all-reduce | flops 1536 | bytes 12288 | tf_op jit(solution)/shard_map/psum | solution.py:122
  481.7 1.5 fusion.23
  (114 shorter events, 7.3 us)
Async XLA Ops:
  6.5 27.8 %copy-start = (bf16[32,128]{1,0:T(8,128)(2,1)S(1)}, bf16[32,128]{1,0:T(8,128)(2,1)}, u32[]{:S(2)}) copy-start(bf16[32,128]{1,0:T(8,128)(2,1)} %param.20) | copy-start | bytes 24580
  6.5 168.4 %all-gather.3.cloned.1.call-start = ((), (), s32[]{:S(2)}) async-start(), calls=%async_computation.2 | async-start | bytes 7077888 | tf_op jit(solution)/shard_map/all_gather | solution.py:75
  7.3 373.5 %all-gather.5.cloned.1.call-start = ((), (), s32[]{:S(2)}) async-start(), calls=%async_computation.3 | async-start | bytes 12976128 | tf_op jit(solution)/shard_map/all_gather | solution.py:113
  11.5 14.8 %copy-start.1 = (bf16[768,512]{1,0:T(8,128)(2,1)S(1)}, bf16[768,512]{1,0:T(8,128)(2,1)}, u32[]{:S(2)}) copy-start(bf16[768,512]{1,0:T(8,128)(2,1)} %param.19) | copy-start | bytes 2359300
  11.5 14.8 %copy-start.2 = (bf16[768,512]{1,0:T(8,128)(2,1)S(1)}, bf16[768,512]{1,0:T(8,128)(2,1)}, u32[]{:S(2)}) copy-start(bf16[768,512]{1,0:T(8,128)(2,1)} %param.18) | copy-start | bytes 2359300
  11.5 154.6 %all-to-all-start = ((bf16[32,512,128]{1,2,0:T(8,128)(2,1)}), bf16[32,512,128]{1,2,0:T(8,128)(2,1)}, u32[]{:S(2)}, u32[]{:S(2)}) async-start(bf16[32,512,128]{1,2,0:T(8,128)(2,1)} %stack.10), calls=%async_computation | async-start | bytes 8388608 | tf_op jit(solution)/shard_map/all_to_all | solution.py:79
  26.3 3.4 copy-start.7
  26.3 437.7 %reduce-scatter.2.cloned.1.call-start = ((), (), s32[]{:S(2)}) async-start(), calls=%async_computation.4 | async-start | bytes 7077888 | tf_op jit(solution)/shard_map/reduce_scatter | solution.py:118
  26.6 36.4 %collective-permute-start = (bf16[128,512]{1,0:T(8,128)(2,1)S(1)}, bf16[128,512]{1,0:T(8,128)(2,1)S(1)}, u32[]{:S(2)}, u32[]{:S(2)}) collective-permute-start(bf16[128,512]{1,0:T(8,128)(2,1)S(1)} %slice.20), channel_id=1, source_target_pairs={{0,8},{8,16},{16,24},{24,32},{32,40},{40,48},{48,56},{56,64},{64,7... | collective-permute-start | bytes 393224 | tf_op jit(solution)/shard_map/ppermute | solution.py:16
  30.3 30.7 %collective-permute-start.1 = (s32[1]{0:T(128)}, s32[1]{0:T(128)}, u32[]{:S(2)}, u32[]{:S(2)}) collective-permute-start(s32[1]{0:T(128)} %bitcast.12), channel_id=1, source_target_pairs={{0,8},{8,16},{16,24},{24,32},{32,40},{40,48},{48,56},{56,64},{64,7... | collective-permute-start | bytes 20 | tf_op jit(solution)/shard_map/ppermute | solution.py:16
  61.7 123.7 %collective-permute-start.3 = (s32[128]{0:T(128)S(1)}, s32[128]{0:T(128)S(1)}, u32[]{:S(2)}, u32[]{:S(2)}) collective-permute-start(s32[128]{0:T(128)S(1)} %slice.19), channel_id=1, source_target_pairs={{8,0},{16,8},{24,16},{32,24},{40,32},{48,40},{56,48},{64,56},{72,6... | collective-permute-start | bytes 1544 | tf_op jit(solution)/shard_map/ppermute | solution.py:16
  183.9 5.7 %collective-permute-start.2 = (bf16[128,512]{1,0:T(8,128)(2,1)S(1)}, bf16[128,512]{1,0:T(8,128)(2,1)S(1)}, u32[]{:S(2)}, u32[]{:S(2)}) collective-permute-start(bf16[128,512]{1,0:T(8,128)(2,1)S(1)} %slice.21), channel_id=1, source_target_pairs={{8,0},{16,8},{24,16},{32,24},{40,32},{48,40},{56,48},{64,56},{72,6... | collective-permute-start | bytes 393224 | tf_op jit(solution)/shard_map/ppermute | solution.py:16
  395.6 0.7 copy-start.6
  395.6 68.4 %copy-start.3 = (bf16[768,512]{1,0:T(8,128)(2,1)S(1)}, bf16[768,512]{1,0:T(8,128)(2,1)}, u32[]{:S(2)}) copy-start(bf16[768,512]{1,0:T(8,128)(2,1)} %param.15) | copy-start | bytes 2359300
  396.2 85.4 %copy-start.4 = (bf16[768,512]{1,0:T(8,128)(2,1)S(1)}, bf16[768,512]{1,0:T(8,128)(2,1)}, u32[]{:S(2)}) copy-start(bf16[768,512]{1,0:T(8,128)(2,1)} %param.14) | copy-start | bytes 2359300
  464.0 17.7 %copy-start.5 = (bf16[768,512]{1,0:T(8,128)(2,1)S(1)}, bf16[768,512]{1,0:T(8,128)(2,1)}, u32[]{:S(2)}) copy-start(bf16[768,512]{1,0:T(8,128)(2,1)} %reduce-scatter.2.cloned.1.call-done) | copy-start | bytes 2359300
Sparse Core Ops, SparseCore 0:
  9.1 165.7 all-gather.2
  178.5 202.2 all-gather.4
  395.7 68.2 reduce-scatter.1
